TPU v7x, 32 devices: a whole 2x2x4 slice. The times are simulated.
32 devices in a mesh: grp: 2 (over y), frm: 8 (over z, x), tp: 2 (over core).
Axes of the slice: x: 2, y: 2, z: 4, core: 2. Of those that a mesh axis runs over, the one named last changes fastest.
Arguments:
- queries: bfloat16 [3072, 2560], P(('grp', 'frm'), 'tp'), parts along dimension 0, may hold values from -60 to 60, as said below
- key_rows: bfloat16 [3072, 2560], P(('grp', 'frm'), 'tp'), parts along dimension 0, may hold values from -60 to 60
- values: bfloat16 [3072, 2560], P(('grp', 'frm'), 'tp'), parts along dimension 0, may hold values from -6 to 6
- query_gain: float32 [2560], P('tp'), may hold values from 0.25 to 1.75
- key_gain: float32 [2560], P('tp'), may hold values from 0.25 to 1.75
- pattern: int32 [16, 4], P(('grp', 'frm')), parts along dimension 0, may hold values 0 or 1
- reference_keys: bfloat16 [64, 2560], P(('grp', 'frm'), 'tp'), parts along dimension 0, may hold values from -6 to 6
- reference_values: bfloat16 [64, 2560], P(('grp', 'frm'), 'tp'), parts along dimension 0, may hold values from -6 to 6
- reference_live: int32 [16], P(('grp', 'frm')), parts along dimension 0, may hold values from 1 to 4
Outputs:
- attention: bfloat16 [3072, 2560], P(('grp', 'frm'), 'tp'), parts along dimension 0
There are 2 independent parts, one for each index of `grp`. A program takes and returns all parts, laid end to end along the dimension named above; an argument that names none is the same for every part. Nothing has to cross between parts.
Inputs may be any that keep to these rules, and one draw needn't show every extreme that they name: `queries`: query entries lie within the range.
All inputs are finite; a program needn't handle non-finite values. No bound on the sum of `pattern` on one device may be relied on, other than what follows from the above.
Results may differ from a plain program's by a relative error of at most 0.012.
The roundings to bfloat16 on the way count: a program that leaves them out, or rounds other values in their place, can miss the bound.
Values may be sent and summed in bfloat16 or wider, within the bound.
No kernel may reach another device: no remote copies, remote signals or barrier semaphores. Data moves between devices by JAX's collectives and lax.ppermute only.
A program may use at most 64 MiB of HBM per device.

v0:
```python
import jax
import jax.numpy as jnp
from jax import lax
from jax.sharding import PartitionSpec as P

HEADS = 20
HEAD_DIM = 128
WINDOW = 2
EPSILON = 1e-06
NEG_FLOOR = -1e30


def passed_along(block, axis, distance):
    devices = range(lax.axis_size(axis))
    route = [((i - distance) % len(devices), i) for i in devices]
    return lax.ppermute(block, axis, route)


def normalize(matrix, scaling, square_sum, features):
    widened = matrix.astype(jnp.float32)
    return (widened * lax.rsqrt(square_sum / features + EPSILON)[:, None] * scaling).astype(
        jnp.bfloat16
    )


def absorb(state, query_part, key_part, value_part, allowed):
    running_max, running_sum, numerator = state
    scaling = query_part.shape[2] ** (-0.5)
    scores = (
        jnp.einsum("thd,nhd->htn", query_part, key_part, preferred_element_type=jnp.float32)
        * scaling
    )
    scores = jnp.where(allowed[None, None, :], scores, -jnp.inf)
    new_max = jnp.maximum(running_max, jnp.max(scores, axis=2))
    weights = jnp.exp(scores - new_max[:, :, None])
    fading = jnp.exp(running_max - new_max)
    running_sum = running_sum * fading + jnp.sum(weights, axis=2)
    numerator = numerator * jnp.transpose(fading)[:, :, None] + jnp.einsum(
        "htn,nhd->thd", weights.astype(jnp.bfloat16), value_part, preferred_element_type=jnp.float32
    )
    return (new_max, running_sum, numerator)


def attend(state, query_heads, key_heads, value_heads, allowed):
    group_width = query_heads.shape[1] // len(state)
    updated = []
    for group_id, group_state in enumerate(state):
        first_head = group_id * group_width
        last_head = first_head + group_width
        updated.append(
            absorb(
                group_state,
                query_heads[:, first_head:last_head],
                key_heads[:, first_head:last_head],
                value_heads[:, first_head:last_head],
                allowed,
            )
        )
    return tuple(updated)


def shards(
    queries,
    key_rows,
    values,
    query_gain,
    key_gain,
    pattern,
    reference_keys,
    reference_values,
    reference_live,
):
    tokens_here, features = queries.shape
    heads_here = features // HEAD_DIM
    squares = lax.psum(
        (
            jnp.sum(jnp.square(queries.astype(jnp.float32)), axis=1),
            jnp.sum(jnp.square(key_rows.astype(jnp.float32)), axis=1),
        ),
        "tp",
    )
    full_width = HEADS * HEAD_DIM
    normed_queries = normalize(queries, query_gain, squares[0], full_width)
    normed_keys = normalize(key_rows, key_gain, squares[1], full_width)
    query_heads = normed_queries.reshape(tokens_here, heads_here, HEAD_DIM)
    own_pair = jnp.stack([normed_keys, values])
    offsets = [column - WINDOW for column in range(WINDOW)] + [
        column + 1 for column in range(WINDOW)
    ]
    arrived = [passed_along(own_pair, "frm", -offset) for offset in offsets]
    groups = 2
    group_width = heads_here // groups
    start_state = tuple(
        (
            (
                jnp.full((group_width, tokens_here), NEG_FLOOR, jnp.float32),
                jnp.zeros((group_width, tokens_here), jnp.float32),
                jnp.zeros((tokens_here, group_width, HEAD_DIM), jnp.float32),
            )
            for group_id in range(groups)
        )
    )
    near_live = pattern[0] > 0

    def split_heads(matrix):
        return matrix.reshape(matrix.shape[0], heads_here, HEAD_DIM)

    every_pair = [own_pair] + arrived
    all_keys = split_heads(jnp.concatenate([key_value[0] for key_value in every_pair], axis=0))
    all_values = split_heads(jnp.concatenate([key_value[1] for key_value in every_pair], axis=0))
    flags = jnp.concatenate([jnp.ones((1,), jnp.bool_), near_live])
    allowed = jnp.repeat(flags, tokens_here)
    row_flags = (jnp.arange(reference_keys.shape[0], dtype=jnp.int32) < reference_live[0]).astype(
        jnp.bfloat16
    )
    pieces = (
        lax.all_gather(reference_keys, "frm", axis=0, tiled=True),
        lax.all_gather(reference_values, "frm", axis=0, tiled=True),
        lax.all_gather(row_flags, "frm", axis=0, tiled=True),
    )
    row_count = pieces[0].shape[0]
    final_state = attend(
        attend(start_state, query_heads, all_keys, all_values, allowed),
        query_heads,
        pieces[0].reshape(row_count, heads_here, HEAD_DIM),
        pieces[1].reshape(row_count, heads_here, HEAD_DIM),
        pieces[2] > 0.5,
    )
    outputs = [
        group_state[2] / jnp.transpose(group_state[1])[:, :, None] for group_state in final_state
    ]
    return jnp.concatenate(outputs, axis=1).reshape(tokens_here, features).astype(jnp.bfloat16)


def solution(mesh):
    in_specs = (
        P(("grp", "frm"), "tp"),
        P(("grp", "frm"), "tp"),
        P(("grp", "frm"), "tp"),
        P("tp"),
        P("tp"),
        P(("grp", "frm"), None),
        P(("grp", "frm"), "tp"),
        P(("grp", "frm"), "tp"),
        P(("grp", "frm")),
    )
    out_specs = P(("grp", "frm"), "tp")
    return jax.shard_map(shards, mesh=mesh, in_specs=in_specs, out_specs=out_specs, check_vma=False)
```

profile of v0, /device:TPU:0, one launch (start us, length us, event | category | flops | bytes accessed | tf_op | source)
XLA Modules:
  0.0 187.1 jit_solution(17618880381193820832)
XLA Ops:
  0.0 1.3 fusion.65
  1.3 1.2 fusion.62
  2.5 2.6 %all-reduce.1 = (f32[192]{0:T(256)S(1)}, f32[192]{0:T(256)S(1)}) all-reduce(f32[192]{0:T(256)S(1)} %fusion.65, f32[192]{0:T(256)S(1)} %fusion.62), channel_id=1, replica_groups=mesh['grp'=2,'frm'=8,'tp'=2] {'tp'}, use_global_device_ids=true, to_apply=%region_3.0 | all-reduce | flops 384 | bytes 3072 | tf_op jit(solution)/shard_map/psum | solution.py:75
  5.1 1.2 fusion.108
  6.3 2.1 %pad_maximum_fusion = bf16[2,192,1280]{2,1,0:T(8,128)(2,1)} fusion(bf16[1,192,1280]{2,1,0:T(8,128)(2,1)} %bitcast.111, bf16[1,192,1280]{2,1,0:T(8,128)(2,1)S(1)} %fusion.108), kind=kLoop, calls=%fused_computation.54 | loop fusion | flops 491520 | bytes 1966080 | tf_op jit(solution)/shard_map/stack | solution.py:86
  8.4 2.9 %collective-permute-start = (bf16[2,192,1280]{2,1,0:T(8,128)(2,1)}, bf16[2,192,1280]{2,1,0:T(8,128)(2,1)}, u32[]{:S(2)}, u32[]{:S(2)}) collective-permute-start(bf16[2,192,1280]{2,1,0:T(8,128)(2,1)} %pad_maximum_fusion), channel_id=1, source_target_pairs={{12,0},{14,2},{0,4},{2,6},{4,8},{6,10},{8,12},{10,14},{13,1},{15,3... | collective-permute-start | bytes 2949128 | tf_op jit(solution)/shard_map/ppermute | solution.py:16
  11.4 1.5 collective-permute-start.1
  12.8 3.2 %collective-permute-start.2 = (bf16[2,192,1280]{2,1,0:T(8,128)(2,1)}, bf16[2,192,1280]{2,1,0:T(8,128)(2,1)S(1)}, u32[]{:S(2)}, u32[]{:S(2)}) collective-permute-start(bf16[2,192,1280]{2,1,0:T(8,128)(2,1)} %pad_maximum_fusion), channel_id=1, source_target_pairs={{2,0},{4,2},{6,4},{8,6},{10,8},{12,10},{14,12},{0,14},{3,1},{5,3},... | collective-permute-start | bytes 2949128 | tf_op jit(solution)/shard_map/ppermute | solution.py:16
  17.1 0.9 constant_dynamic-update-slice_fusion.9
  20.2 82.3 %all-gather = bf16[8,4,1280]{2,1,0:T(4,128)(2,1)S(1)} all-gather(bf16[1,4,1280]{2,1,0:T(4,128)(2,1)S(1)} %bitcast.112), channel_id=1, replica_groups=mesh['grp'=2,'frm'=8,'tp'=2] {'frm'}, dimensions={0}, use_global_device_ids=true | all-gather | bytes 92160 | tf_op jit(solution)/shard_map/all_gather | solution.py:117
  104.7 18.7 %all-reduce = bf16[32]{0:T(256)(128)(2,1)S(1)} all-reduce(bf16[32]{0:T(256)(128)(2,1)S(1)} %dynamic-update-slice), channel_id=1, replica_groups=mesh['grp'=2,'frm'=8,'tp'=2] {'frm'}, use_global_device_ids=true, to_apply=%add | all-reduce | flops 32 | bytes 128
  123.4 30.7 %all-gather.1 = bf16[8,4,1280]{2,1,0:T(4,128)(2,1)S(1)} all-gather(bf16[1,4,1280]{2,1,0:T(4,128)(2,1)S(1)} %bitcast.113), channel_id=1, replica_groups=mesh['grp'=2,'frm'=8,'tp'=2] {'frm'}, dimensions={0}, use_global_device_ids=true | all-gather | bytes 92160 | tf_op jit(solution)/shard_map/all_gather | solution.py:118
  155.9 2.0 %fusion.99 = (bf16[1,192,1280]{2,1,0:T(8,128)(2,1)}, bf16[1,192,1280]{2,1,0:T(8,128)(2,1)S(1)}) fusion(bf16[2,192,1280]{2,1,0:T(8,128)(2,1)} %collective-permute-done), kind=kLoop, calls=%fused_computation.111 | loop fusion | bytes 1966080 | tf_op jit(solution)/shard_map/slice | solution.py:109
  158.5 2.0 %fusion.98 = (bf16[1,192,1280]{2,1,0:T(8,128)(2,1)}, bf16[1,192,1280]{2,1,0:T(8,128)(2,1)S(1)}) fusion(bf16[2,192,1280]{2,1,0:T(8,128)(2,1)} %collective-permute-done.1), kind=kLoop, calls=%fused_computation.110 | loop fusion | bytes 1966080 | tf_op jit(solution)/shard_map/slice | solution.py:109
  162.5 2.0 %fusion.96 = (bf16[1,192,1280]{2,1,0:T(8,128)(2,1)}, bf16[1,192,1280]{2,1,0:T(8,128)(2,1)S(1)}) fusion(bf16[2,192,1280]{2,1,0:T(8,128)(2,1)} %collective-permute-done.3), kind=kLoop, calls=%fused_computation.108 | loop fusion | bytes 1966080 | tf_op jit(solution)/shard_map/slice | solution.py:109
  165.1 1.3 copy.42
  166.4 1.0 copy.47
  167.4 1.3 copy.43
  168.7 1.0 copy.48
  169.7 1.3 copy.44
  170.9 1.1 copy.49
  172.0 1.3 copy.45
  173.3 1.0 copy.50
  174.3 0.9 constant_dynamic-update-slice_fusion.8
  175.2 0.9 constant_dynamic-update-slice_fusion.7
  176.1 0.9 constant_dynamic-update-slice_fusion.6
  178.2 1.1 fusion
  179.3 1.9 %fusion.2 = (f32[5,192]{1,0:T(8,128)S(1)}, f32[5,192]{1,0:T(8,128)S(1)}, f32[5,192,960]{2,1,0:T(8,128)S(1)}) fusion(f32[5,192,960]{2,1,0:T(8,128)S(1)} %get-tuple-element.36, f32[5,192]{1,0:T(8,128)S(1)} %get-tuple-element.27, pred[960]{0:T(1024)(128)(4,1)S(1)} %broadcast_in_dim.54, bf16[192,10,128]{0,2,1:T(8,128)(2,1)S(1)} %bitcast.99, ...), kind=kOutput, calls=%fused_computation.6 | convolution fusion | flops 242378880 | bytes 9519616 | tf_op jit(solution)/shard_map/thd,nhd->htn/dot_general | solution.py:30
  181.3 1.0 fusion.4
  182.9 1.1 fusion.53
  184.0 1.1 fusion.48
  186.1 1.0 copy.67
  (87 shorter events, 11.6 us)
Async XLA Ops:
  0.0 16.6 %copy-start = (bf16[192,1280]{1,0:T(8,128)(2,1)S(1)}, bf16[192,1280]{1,0:T(8,128)(2,1)}, u32[]{:S(2)}) copy-start(bf16[192,1280]{1,0:T(8,128)(2,1)} %param.10) | copy-start | bytes 1474564
  0.0 16.6 %copy-start.11 = (f32[1280]{0:T(1024)S(1)}, f32[1280]{0:T(1024)}, u32[]{:S(2)}) copy-start(f32[1280]{0:T(1024)} %param.13) | copy-start | bytes 15364
  0.0 16.4 %copy-start.6 = (bf16[192,1280]{1,0:T(8,128)(2,1)S(1)}, bf16[192,1280]{1,0:T(8,128)(2,1)}, u32[]{:S(2)}) copy-start(bf16[192,1280]{1,0:T(8,128)(2,1)} %param.11) | copy-start | bytes 1474564
  8.4 9.6 %copy-start.15 = (s32[1,4]{1,0:T(1,128)S(1)}, s32[1,4]{1,0:T(1,128)}, u32[]{:S(2)}) copy-start(s32[1,4]{1,0:T(1,128)} %param.14) | copy-start | bytes 52
  8.4 9.9 %copy-start.1 = (bf16[192,1280]{1,0:T(8,128)(2,1)S(1)}, bf16[192,1280]{1,0:T(8,128)(2,1)}, u32[]{:S(2)}) copy-start(bf16[192,1280]{1,0:T(8,128)(2,1)} %param.9) | copy-start | bytes 1474564
  8.4 9.9 %copy-start.14 = (f32[1280]{0:T(1024)S(1)}, f32[1280]{0:T(1024)}, u32[]{:S(2)}) copy-start(f32[1280]{0:T(1024)} %param.12) | copy-start | bytes 15364
  8.4 147.5 %collective-permute-start = (bf16[2,192,1280]{2,1,0:T(8,128)(2,1)}, bf16[2,192,1280]{2,1,0:T(8,128)(2,1)}, u32[]{:S(2)}, u32[]{:S(2)}) collective-permute-start(bf16[2,192,1280]{2,1,0:T(8,128)(2,1)} %pad_maximum_fusion), channel_id=1, source_target_pairs={{12,0},{14,2},{0,4},{2,6},{4,8},{6,10},{8,12},{10,14},{13,1},{15,3... | collective-permute-start | bytes 2949128 | tf_op jit(solution)/shard_map/ppermute | solution.py:16
  11.4 147.2 %collective-permute-start.1 = (bf16[2,192,1280]{2,1,0:T(8,128)(2,1)}, bf16[2,192,1280]{2,1,0:T(8,128)(2,1)}, u32[]{:S(2)}, u32[]{:S(2)}) collective-permute-start(bf16[2,192,1280]{2,1,0:T(8,128)(2,1)} %pad_maximum_fusion), channel_id=1, source_target_pairs={{14,0},{0,2},{2,4},{4,6},{6,8},{8,10},{10,12},{12,14},{15,1},{1,3}... | collective-permute-start | bytes 2949128 | tf_op jit(solution)/shard_map/ppermute | solution.py:16
  12.8 148.3 %collective-permute-start.2 = (bf16[2,192,1280]{2,1,0:T(8,128)(2,1)}, bf16[2,192,1280]{2,1,0:T(8,128)(2,1)S(1)}, u32[]{:S(2)}, u32[]{:S(2)}) collective-permute-start(bf16[2,192,1280]{2,1,0:T(8,128)(2,1)} %pad_maximum_fusion), channel_id=1, source_target_pairs={{2,0},{4,2},{6,4},{8,6},{10,8},{12,10},{14,12},{0,14},{3,1},{5,3},... | collective-permute-start | bytes 2949128 | tf_op jit(solution)/shard_map/ppermute | solution.py:16
  16.1 146.5 %collective-permute-start.3 = (bf16[2,192,1280]{2,1,0:T(8,128)(2,1)}, bf16[2,192,1280]{2,1,0:T(8,128)(2,1)}, u32[]{:S(2)}, u32[]{:S(2)}) collective-permute-start(bf16[2,192,1280]{2,1,0:T(8,128)(2,1)} %pad_maximum_fusion), channel_id=1, source_target_pairs={{4,0},{6,2},{8,4},{10,6},{12,8},{14,10},{0,12},{2,14},{5,1},{7,3},... | collective-permute-start | bytes 2949128 | tf_op jit(solution)/shard_map/ppermute | solution.py:16
  18.5 1.7 copy-start.12
  18.5 84.6 %copy-start.16 = (u32[32]{0:T(128)S(1)}, u32[32]{0:T(128)}, u32[]{:S(2)}) copy-start(u32[32]{0:T(128)} %constant.29) | copy-start | bytes 388
  18.5 104.9 %copy-start.13 = (bf16[4,1280]{1,0:T(4,128)(2,1)S(1)}, bf16[4,1280]{1,0:T(4,128)(2,1)}, u32[]{:S(2)}) copy-start(bf16[4,1280]{1,0:T(4,128)(2,1)} %param.16) | copy-start | bytes 30724
  174.3 3.6 %copy-start.2 = (bf16[192,10,128]{2,0,1:T(8,128)(2,1)S(1)}, bf16[192,10,128]{2,0,1:T(8,128)(2,1)}, u32[]{:S(2)}) copy-start(bf16[192,10,128]{2,0,1:T(8,128)(2,1)} %copy.47) | copy-start | bytes 1474564
  174.3 3.6 %copy-start.9 = (bf16[960,10,128]{2,0,1:T(8,128)(2,1)S(1)}, bf16[960,10,128]{2,0,1:T(8,128)(2,1)}, u32[]{:S(2)}) copy-start(bf16[960,10,128]{2,0,1:T(8,128)(2,1)} %constant_dynamic-update-slice_fusion.4) | copy-start | bytes 7372804
  174.3 3.7 %copy-start.3 = (bf16[192,10,128]{2,0,1:T(8,128)(2,1)S(1)}, bf16[192,10,128]{2,0,1:T(8,128)(2,1)}, u32[]{:S(2)}) copy-start(bf16[192,10,128]{2,0,1:T(8,128)(2,1)} %copy.48) | copy-start | bytes 1474564
  175.2 2.9 %copy-start.4 = (bf16[192,10,128]{2,0,1:T(8,128)(2,1)S(1)}, bf16[192,10,128]{2,0,1:T(8,128)(2,1)}, u32[]{:S(2)}) copy-start(bf16[192,10,128]{2,0,1:T(8,128)(2,1)} %copy.49) | copy-start | bytes 1474564
  176.1 2.0 %copy-start.5 = (bf16[192,10,128]{2,0,1:T(8,128)(2,1)S(1)}, bf16[192,10,128]{2,0,1:T(8,128)(2,1)}, u32[]{:S(2)}) copy-start(bf16[192,10,128]{2,0,1:T(8,128)(2,1)} %copy.50) | copy-start | bytes 1474564
  179.3 1.9 %copy-start.7 = (f32[5,192,32]{1,2,0:T(8,128)S(1)}, f32[5,192,32]{1,2,0:T(8,128)}, u32[]{:S(2)}) copy-start(f32[5,192,32]{1,2,0:T(8,128)} %get-tuple-element.32) | copy-start | bytes 368644
  181.2 1.7 copy-start.8
  184.0 1.1 copy-start.10
where the time goes:
time: 188 us; the launch traced here: 187 us
  blocking collectives  134 us (71%)
  local copies, waits for them, and re-layouts  28.9 us (15%)
  starting transfers between devices  7.92 us (4%)
  other arithmetic  7.48 us (4%)
  matrix products  6.85 us (4%)
    all_gather x1, blocking collectives, shards(): lax.all_gather(reference_keys, 'frm', axis=0, tiled=True)  82.3 us
    all_gather x1, blocking collectives, shards(): lax.all_gather(reference_values, 'frm', axis=0, tiled=True)  30.7 us
    unnamed x1, blocking collectives  18.7 us
    slice x8, local copies, waits for them, and re-layouts, shards(): key_value[0]  12 us
    ppermute x4, starting transfers between devices, passed_along(): return lax.ppermute(block, axis, route)  7.92 us
    unnamed x46, local copies, waits for them, and re-layouts  6.38 us
    concatenate x6, local copies, waits for them, and re-layouts, shards(): jnp.concatenate([key_value[0] for key_value in every_pair], axis=0)  4.48 us
    dot_general x4, matrix products, absorb(): jnp.einsum('thd,nhd->htn', query_part, key_part, preferred_element_type=j...  4 us
  transfers between devices with their start and end apart: 4, of which 0 were waited for; matrix products, arithmetic and copies ran while one was open for 7% of the time, Pallas kernels for 0%

commit v1 on v0

--- a/solution.py
+++ b/solution.py
@@ -8,6 +8,18 @@
 WINDOW = 2
 EPSILON = 1e-06
 NEG_FLOOR = -1e30
+
+
+def gather_by_bits(value, axis, dim):
+    ways, here = (lax.axis_size(axis), lax.axis_index(axis))
+    grown, reach = (value, 1)
+    while reach < ways:
+        theirs = lax.ppermute(grown, axis, [(d, d ^ reach) for d in range(ways)])
+        mine_first = jnp.concatenate([grown, theirs], axis=dim)
+        theirs_first = jnp.concatenate([theirs, grown], axis=dim)
+        grown = jnp.where(here & reach == 0, mine_first, theirs_first)
+        reach = 2 * reach
+    return grown
 
 
 def passed_along(block, axis, distance):
@@ -115,7 +127,7 @@
     )
     pieces = (
         lax.all_gather(reference_keys, "frm", axis=0, tiled=True),
-        lax.all_gather(reference_values, "frm", axis=0, tiled=True),
+        gather_by_bits(reference_values, "frm", 0),
         lax.all_gather(row_flags, "frm", axis=0, tiled=True),
     )
     row_count = pieces[0].shape[0]

time: 188 us -> 166 us (0.88)
  blocking collectives: 134 us -> 104 us
  waiting for transfers between devices: 0.01 us -> 8.62 us
    all_gather x1 -> x0, blocking collectives: 30.7 us -> none  [shards(): lax.all_gather(reference_values, 'frm', axis=0, tiled=True)]
    ppermute x0 -> x3, waiting for transfers between devices: none -> 8.61 us  [gather_by_bits(): theirs = lax.ppermute(grown, axis, [(d, d ^ reach) for d in range(ways)])]
    unnamed x46 -> x44, local copies, waits for them, and re-layouts: 6.38 us -> 6.28 us
  transfers between devices with their start and end apart: 4 -> 7, of which waited for: 0 -> 2; matrix products, arithmetic and copies ran while one was open for 7% -> 7% of each run, Pallas kernels for 0% -> 0%
where the time goes in v1:
time: 166 us; the launch traced here: 165 us
  blocking collectives  104 us (63%)
  local copies, waits for them, and re-layouts  28.1 us (17%)
  starting transfers between devices  8.81 us (5%)
  waiting for transfers between devices  8.62 us (5%)
  other arithmetic  7.56 us (5%)
  matrix products  6.81 us (4%)
  between operations  1.76 us (1%)
    all_gather x1, blocking collectives, shards(): lax.all_gather(reference_keys, 'frm', axis=0, tiled=True)  82.2 us
    unnamed x1, blocking collectives  18.9 us
    slice x8, local copies, waits for them, and re-layouts, shards(): key_value[0]  12 us
    ppermute x3, waiting for transfers between devices, gather_by_bits(): theirs = lax.ppermute(grown, axis, [(d, d ^ reach) for d in range(ways)])  8.61 us
    ppermute x4, starting transfers between devices, passed_along(): return lax.ppermute(block, axis, route)  7.89 us
    unnamed x44, local copies, waits for them, and re-layouts  6.28 us
    concatenate x6, local copies, waits for them, and re-layouts, shards(): jnp.concatenate([key_value[0] for key_value in every_pair], axis=0)  4.49 us
    dot_general x4, matrix products, absorb(): jnp.einsum('thd,nhd->htn', query_part, key_part, preferred_element_type=j...  4 us
  transfers between devices with their start and end apart: 7, of which 2 were waited for; matrix products, arithmetic and copies ran while one was open for 7% of the time, Pallas kernels for 0%

profile of v1, /device:TPU:0, one launch (start us, length us, event | category | flops | bytes accessed | tf_op | source)
XLA Modules:
  0.0 165.4 jit_solution(15596802892050658033)
XLA Ops:
  0.0 1.3 fusion.65
  1.3 1.2 fusion.62
  2.5 2.6 %all-reduce.1 = (f32[192]{0:T(256)S(1)}, f32[192]{0:T(256)S(1)}) all-reduce(f32[192]{0:T(256)S(1)} %fusion.65, f32[192]{0:T(256)S(1)} %fusion.62), channel_id=1, replica_groups=mesh['grp'=2,'frm'=8,'tp'=2] {'tp'}, use_global_device_ids=true, to_apply=%region_3.0 | all-reduce | flops 384 | bytes 3072 | tf_op jit(solution)/shard_map/psum | solution.py:87
  5.1 1.2 fusion.107
  6.4 2.1 %pad_maximum_fusion = bf16[2,192,1280]{2,1,0:T(8,128)(2,1)} fusion(bf16[1,192,1280]{2,1,0:T(8,128)(2,1)} %bitcast.118, bf16[1,192,1280]{2,1,0:T(8,128)(2,1)S(1)} %fusion.107), kind=kLoop, calls=%fused_computation.54 | loop fusion | flops 491520 | bytes 1966080 | tf_op jit(solution)/shard_map/stack | solution.py:98
  8.5 2.9 %collective-permute-start = (bf16[2,192,1280]{2,1,0:T(8,128)(2,1)}, bf16[2,192,1280]{2,1,0:T(8,128)(2,1)}, u32[]{:S(2)}, u32[]{:S(2)}) collective-permute-start(bf16[2,192,1280]{2,1,0:T(8,128)(2,1)} %pad_maximum_fusion), channel_id=1, source_target_pairs={{12,0},{14,2},{0,4},{2,6},{4,8},{6,10},{8,12},{10,14},{13,1},{15,3... | collective-permute-start | bytes 2949128 | tf_op jit(solution)/shard_map/ppermute | solution.py:28
  11.4 1.5 collective-permute-start.1
  12.9 3.2 %collective-permute-start.2 = (bf16[2,192,1280]{2,1,0:T(8,128)(2,1)}, bf16[2,192,1280]{2,1,0:T(8,128)(2,1)S(1)}, u32[]{:S(2)}, u32[]{:S(2)}) collective-permute-start(bf16[2,192,1280]{2,1,0:T(8,128)(2,1)} %pad_maximum_fusion), channel_id=1, source_target_pairs={{2,0},{4,2},{6,4},{8,6},{10,8},{12,10},{14,12},{0,14},{3,1},{5,3},... | collective-permute-start | bytes 2949128 | tf_op jit(solution)/shard_map/ppermute | solution.py:28
  19.4 0.9 constant_dynamic-update-slice_fusion.4
  20.3 82.2 %all-gather = bf16[8,4,1280]{2,1,0:T(4,128)(2,1)S(1)} all-gather(bf16[1,4,1280]{2,1,0:T(4,128)(2,1)S(1)} %bitcast.122), channel_id=1, replica_groups=mesh['grp'=2,'frm'=8,'tp'=2] {'frm'}, dimensions={0}, use_global_device_ids=true | all-gather | bytes 92160 | tf_op jit(solution)/shard_map/all_gather | solution.py:129
  105.2 18.9 %all-reduce = bf16[32]{0:T(256)(128)(2,1)S(1)} all-reduce(bf16[32]{0:T(256)(128)(2,1)S(1)} %dynamic-update-slice), channel_id=1, replica_groups=mesh['grp'=2,'frm'=8,'tp'=2] {'frm'}, use_global_device_ids=true, to_apply=%add | all-reduce | flops 32 | bytes 128
  125.5 3.7 %collective-permute-done.5 = bf16[8,1280]{1,0:T(8,128)(2,1)S(1)} collective-permute-done((bf16[8,1280]{1,0:T(8,128)(2,1)S(1)}, bf16[8,1280]{1,0:T(8,128)(2,1)S(1)}, u32[]{:S(2)}, u32[]{:S(2)}) %collective-permute-start.5) | collective-permute-done | bytes 20512 | tf_op jit(solution)/shard_map/ppermute | solution.py:17
  129.4 4.9 %collective-permute-done.6 = bf16[16,1280]{1,0:T(8,128)(2,1)S(1)} collective-permute-done((bf16[16,1280]{1,0:T(8,128)(2,1)S(1)}, bf16[16,1280]{1,0:T(8,128)(2,1)S(1)}, u32[]{:S(2)}, u32[]{:S(2)}) %collective-permute-start.6) | collective-permute-done | bytes 40992 | tf_op jit(solution)/shard_map/ppermute | solution.py:17
  134.3 2.0 %fusion.99 = (bf16[1,192,1280]{2,1,0:T(8,128)(2,1)}, bf16[1,192,1280]{2,1,0:T(8,128)(2,1)S(1)}) fusion(bf16[2,192,1280]{2,1,0:T(8,128)(2,1)} %collective-permute-done), kind=kLoop, calls=%fused_computation.117 | loop fusion | bytes 1966080 | tf_op jit(solution)/shard_map/slice | solution.py:121
  136.8 2.1 %fusion.98 = (bf16[1,192,1280]{2,1,0:T(8,128)(2,1)}, bf16[1,192,1280]{2,1,0:T(8,128)(2,1)S(1)}) fusion(bf16[2,192,1280]{2,1,0:T(8,128)(2,1)} %collective-permute-done.1), kind=kLoop, calls=%fused_computation.116 | loop fusion | bytes 1966080 | tf_op jit(solution)/shard_map/slice | solution.py:121
  140.9 2.0 %fusion.96 = (bf16[1,192,1280]{2,1,0:T(8,128)(2,1)}, bf16[1,192,1280]{2,1,0:T(8,128)(2,1)S(1)}) fusion(bf16[2,192,1280]{2,1,0:T(8,128)(2,1)} %collective-permute-done.3), kind=kLoop, calls=%fused_computation.114 | loop fusion | bytes 1966080 | tf_op jit(solution)/shard_map/slice | solution.py:121
  143.4 1.3 copy.42
  144.7 1.0 copy.47
  145.7 1.3 copy.43
  147.0 1.0 copy.48
  148.0 1.3 copy.44
  149.3 1.1 copy.49
  150.4 1.3 copy.45
  151.6 1.0 copy.50
  152.6 0.9 constant_dynamic-update-slice_fusion.8
  153.5 0.9 constant_dynamic-update-slice_fusion.7
  156.5 1.1 fusion
  157.6 1.9 %fusion.2 = (f32[5,192]{1,0:T(8,128)S(1)}, f32[5,192]{1,0:T(8,128)S(1)}, f32[5,192,960]{2,1,0:T(8,128)S(1)}) fusion(f32[5,192,960]{2,1,0:T(8,128)S(1)} %get-tuple-element.34, f32[5,192]{1,0:T(8,128)S(1)} %get-tuple-element.25, pred[960]{0:T(1024)(128)(4,1)S(1)} %broadcast_in_dim.54, bf16[192,10,128]{0,2,1:T(8,128)(2,1)S(1)} %bitcast.106, ...), kind=kOutput, calls=%fused_computation.6 | convolution fusion | flops 242378880 | bytes 9519616 | tf_op jit(solution)/shard_map/thd,nhd->htn/dot_general | solution.py:42
  159.6 1.0 fusion.4
  161.2 1.1 fusion.53
  162.3 1.1 fusion.48
  164.4 1.0 copy.67
  (93 shorter events, 12.7 us)
Async XLA Ops:
  0.0 17.4 %copy-start = (bf16[192,1280]{1,0:T(8,128)(2,1)S(1)}, bf16[192,1280]{1,0:T(8,128)(2,1)}, u32[]{:S(2)}) copy-start(bf16[192,1280]{1,0:T(8,128)(2,1)} %param.10) | copy-start | bytes 1474564
  0.0 17.4 %copy-start.11 = (f32[1280]{0:T(1024)S(1)}, f32[1280]{0:T(1024)}, u32[]{:S(2)}) copy-start(f32[1280]{0:T(1024)} %param.13) | copy-start | bytes 15364
  0.0 17.1 %copy-start.6 = (bf16[192,1280]{1,0:T(8,128)(2,1)S(1)}, bf16[192,1280]{1,0:T(8,128)(2,1)}, u32[]{:S(2)}) copy-start(bf16[192,1280]{1,0:T(8,128)(2,1)} %param.11) | copy-start | bytes 1474564
  0.0 16.3 %copy-start.10 = (bf16[4,1280]{1,0:T(4,128)(2,1)S(1)}, bf16[4,1280]{1,0:T(4,128)(2,1)}, u32[]{:S(2)}) copy-start(bf16[4,1280]{1,0:T(4,128)(2,1)} %param.16) | copy-start | bytes 30724
  8.4 10.4 %copy-start.14 = (s32[1,4]{1,0:T(1,128)S(1)}, s32[1,4]{1,0:T(1,128)}, u32[]{:S(2)}) copy-start(s32[1,4]{1,0:T(1,128)} %param.14) | copy-start | bytes 52
  8.5 125.8 %collective-permute-start = (bf16[2,192,1280]{2,1,0:T(8,128)(2,1)}, bf16[2,192,1280]{2,1,0:T(8,128)(2,1)}, u32[]{:S(2)}, u32[]{:S(2)}) collective-permute-start(bf16[2,192,1280]{2,1,0:T(8,128)(2,1)} %pad_maximum_fusion), channel_id=1, source_target_pairs={{12,0},{14,2},{0,4},{2,6},{4,8},{6,10},{8,12},{10,14},{13,1},{15,3... | collective-permute-start | bytes 2949128 | tf_op jit(solution)/shard_map/ppermute | solution.py:28
  11.4 125.5 %collective-permute-start.1 = (bf16[2,192,1280]{2,1,0:T(8,128)(2,1)}, bf16[2,192,1280]{2,1,0:T(8,128)(2,1)}, u32[]{:S(2)}, u32[]{:S(2)}) collective-permute-start(bf16[2,192,1280]{2,1,0:T(8,128)(2,1)} %pad_maximum_fusion), channel_id=1, source_target_pairs={{14,0},{0,2},{2,4},{4,6},{6,8},{8,10},{10,12},{12,14},{15,1},{1,3}... | collective-permute-start | bytes 2949128 | tf_op jit(solution)/shard_map/ppermute | solution.py:28
  12.9 126.6 %collective-permute-start.2 = (bf16[2,192,1280]{2,1,0:T(8,128)(2,1)}, bf16[2,192,1280]{2,1,0:T(8,128)(2,1)S(1)}, u32[]{:S(2)}, u32[]{:S(2)}) collective-permute-start(bf16[2,192,1280]{2,1,0:T(8,128)(2,1)} %pad_maximum_fusion), channel_id=1, source_target_pairs={{2,0},{4,2},{6,4},{8,6},{10,8},{12,10},{14,12},{0,14},{3,1},{5,3},... | collective-permute-start | bytes 2949128 | tf_op jit(solution)/shard_map/ppermute | solution.py:28
  16.1 124.8 %collective-permute-start.3 = (bf16[2,192,1280]{2,1,0:T(8,128)(2,1)}, bf16[2,192,1280]{2,1,0:T(8,128)(2,1)}, u32[]{:S(2)}, u32[]{:S(2)}) collective-permute-start(bf16[2,192,1280]{2,1,0:T(8,128)(2,1)} %pad_maximum_fusion), channel_id=1, source_target_pairs={{4,0},{6,2},{8,4},{10,6},{12,8},{14,10},{0,12},{2,14},{5,1},{7,3},... | collective-permute-start | bytes 2949128 | tf_op jit(solution)/shard_map/ppermute | solution.py:28
  16.3 109.0 %collective-permute-start.4 = (bf16[4,1280]{1,0:T(4,128)(2,1)S(1)}, bf16[4,1280]{1,0:T(4,128)(2,1)S(1)}, u32[]{:S(2)}, u32[]{:S(2)}) collective-permute-start(bf16[4,1280]{1,0:T(4,128)(2,1)S(1)} %copy-done.10), channel_id=1, source_target_pairs={{0,2},{2,0},{4,6},{6,4},{8,10},{10,8},{12,14},{14,12},{1,3},{3,1},... | collective-permute-start | bytes 30728 | tf_op jit(solution)/shard_map/ppermute | solution.py:17
  17.6 2.7 %copy-start.12 = (bf16[4,1280]{1,0:T(4,128)(2,1)S(1)}, bf16[4,1280]{1,0:T(4,128)(2,1)}, u32[]{:S(2)}) copy-start(bf16[4,1280]{1,0:T(4,128)(2,1)} %param.15) | copy-start | bytes 30724
  17.9 85.3 %copy-start.1 = (bf16[192,1280]{1,0:T(8,128)(2,1)S(1)}, bf16[192,1280]{1,0:T(8,128)(2,1)}, u32[]{:S(2)}) copy-start(bf16[192,1280]{1,0:T(8,128)(2,1)} %param.9) | copy-start | bytes 1474564
  17.9 85.3 %copy-start.13 = (f32[1280]{0:T(1024)S(1)}, f32[1280]{0:T(1024)}, u32[]{:S(2)}) copy-start(f32[1280]{0:T(1024)} %param.12) | copy-start | bytes 15364
  18.8 84.6 %copy-start.15 = (u32[32]{0:T(128)S(1)}, u32[32]{0:T(128)}, u32[]{:S(2)}) copy-start(u32[32]{0:T(128)} %constant.42) | copy-start | bytes 388
  125.4 3.8 %collective-permute-start.5 = (bf16[8,1280]{1,0:T(8,128)(2,1)S(1)}, bf16[8,1280]{1,0:T(8,128)(2,1)S(1)}, u32[]{:S(2)}, u32[]{:S(2)}) collective-permute-start(bf16[8,1280]{1,0:T(8,128)(2,1)S(1)} %maximum_select_fusion.4), channel_id=1, source_target_pairs={{0,4},{2,6},{4,0},{6,2},{8,12},{10,14},{12,8},{14,10},{1,5},{3,7},... | collective-permute-start | bytes 61448 | tf_op jit(solution)/shard_map/ppermute | solution.py:17
  129.3 5.0 %collective-permute-start.6 = (bf16[16,1280]{1,0:T(8,128)(2,1)S(1)}, bf16[16,1280]{1,0:T(8,128)(2,1)S(1)}, u32[]{:S(2)}, u32[]{:S(2)}) collective-permute-start(bf16[16,1280]{1,0:T(8,128)(2,1)S(1)} %maximum_select_fusion.2), channel_id=1, source_target_pairs={{0,8},{2,10},{4,12},{6,14},{8,0},{10,2},{12,4},{14,6},{1,9},{3,11}... | collective-permute-start | bytes 122888 | tf_op jit(solution)/shard_map/ppermute | solution.py:17
  152.6 3.6 %copy-start.2 = (bf16[192,10,128]{2,0,1:T(8,128)(2,1)S(1)}, bf16[192,10,128]{2,0,1:T(8,128)(2,1)}, u32[]{:S(2)}) copy-start(bf16[192,10,128]{2,0,1:T(8,128)(2,1)} %copy.47) | copy-start | bytes 1474564
  152.6 3.6 %copy-start.8 = (bf16[960,10,128]{2,0,1:T(8,128)(2,1)S(1)}, bf16[960,10,128]{2,0,1:T(8,128)(2,1)}, u32[]{:S(2)}) copy-start(bf16[960,10,128]{2,0,1:T(8,128)(2,1)} %constant_dynamic-update-slice_fusion.4) | copy-start | bytes 7372804
  152.6 3.6 %copy-start.3 = (bf16[192,10,128]{2,0,1:T(8,128)(2,1)S(1)}, bf16[192,10,128]{2,0,1:T(8,128)(2,1)}, u32[]{:S(2)}) copy-start(bf16[192,10,128]{2,0,1:T(8,128)(2,1)} %copy.48) | copy-start | bytes 1474564
  153.5 2.8 %copy-start.4 = (bf16[192,10,128]{2,0,1:T(8,128)(2,1)S(1)}, bf16[192,10,128]{2,0,1:T(8,128)(2,1)}, u32[]{:S(2)}) copy-start(bf16[192,10,128]{2,0,1:T(8,128)(2,1)} %copy.49) | copy-start | bytes 1474564
  154.4 2.0 %copy-start.5 = (bf16[192,10,128]{2,0,1:T(8,128)(2,1)S(1)}, bf16[192,10,128]{2,0,1:T(8,128)(2,1)}, u32[]{:S(2)}) copy-start(bf16[192,10,128]{2,0,1:T(8,128)(2,1)} %copy.50) | copy-start | bytes 1474564
  157.6 1.9 %copy-start.7 = (f32[5,192,32]{1,2,0:T(8,128)S(1)}, f32[5,192,32]{1,2,0:T(8,128)}, u32[]{:S(2)}) copy-start(f32[5,192,32]{1,2,0:T(8,128)} %get-tuple-element.30) | copy-start | bytes 368644
  159.5 1.7 %copy-start.9 = (bf16[960,10,128]{2,0,1:T(8,128)(2,1)S(1)}, bf16[960,10,128]{2,0,1:T(8,128)(2,1)}, u32[]{:S(2)}) copy-start(bf16[960,10,128]{2,0,1:T(8,128)(2,1)} %constant_dynamic-update-slice_fusion.5) | copy-start | bytes 7372804
